TPU v7x, 32 devices: a whole 2x2x4 slice. The times are simulated.
32 devices in a mesh: grp: 4 (over y, x), tile: 8 (over z, core).
Axes of the slice: x: 2, y: 2, z: 4, core: 2. Of those that a mesh axis runs over, the one named last changes fastest.
Arguments:
- observed: bfloat16 [512, 32, 2048], P('tile', 'grp'), as said below
- visible: int32 [32, 2048], P('grp', 'tile'), may hold values from 0 to 65535
- params_start: float32 [8, 32, 2048], P(None, 'grp', 'tile'), may hold values from -1.5 to 1.5, as said below
- light_directions: float32 [3, 32], replicated, may hold values from -1 to 1
- view_dirs: float32 [3, 16], replicated, may hold values from -1 to 1
- gains_start: float32 [32], replicated, may hold values from 0.5 to 1.5
Outputs:
- params_out: float32 [8, 32, 2048], P(None, 'grp', 'tile')
- gains_out: float32 [32], replicated
Inputs may be any that keep to these rules, and one draw needn't show every extreme that they name: `observed`: luminance is positive. `params_start`: tilts within -0.3 to 0.3, diffuse 0.3 to 1.2, specular 0.1 to 0.8, sharpness logit -1.5 to 1.5, ambient -0.2 to 0.3, rim 0 to 0.5, retro -0.3 to 0.3.
All inputs are finite; a program needn't handle non-finite values.
Results may differ from a plain program's by a relative error of at most 0.0003.
Values may be sent and summed in bfloat16 or wider, within the bound.
No kernel may reach another device: no remote copies, remote signals or barrier semaphores. Data moves between devices by JAX's collectives and lax.ppermute only.
A program may use at most 64 MiB of HBM per device.

v0:
```python
import jax
import jax.numpy as jnp
from jax import lax
from jax.sharding import PartitionSpec as P

CAMS = 16
LIGHTS = 32
ITERS = 2
damping = 4.0
lift_z = 1.6


def padded_2(cells, sides, width):
    for axis, dim in sides:
        count = lax.axis_size(axis)
        ends = count - 1
        head = lax.slice_in_dim(cells, 0, width, axis=dim)
        tail = lax.slice_in_dim(cells, cells.shape[dim] - width, cells.shape[dim], axis=dim)
        cells = jnp.concatenate(
            [
                lax.ppermute(tail, axis, [(i, (i + 1) % count) for i in range(ends)]),
                cells,
                lax.ppermute(head, axis, [((i + 1) % count, i) for i in range(ends)]),
            ],
            axis=dim,
        )
    return cells


def unit_columns(raw):
    lifted = raw + jnp.array([0.0, 0.0, lift_z], jnp.float32)[:, None]
    return lifted / jnp.sqrt(jnp.sum(lifted * lifted, axis=0, keepdims=True))


def geometry(light_directions, view_dirs):
    lights = unit_columns(light_directions)
    views = unit_columns(view_dirs)
    raw_half = views.T[:, :, None] + lights[None]
    halves = raw_half / jnp.sqrt(jnp.sum(raw_half * raw_half, axis=1, keepdims=True))
    echoes = jnp.sum(views.T[:, :, None] * lights[None], axis=1)
    return (lights, halves, views.T, echoes)


def facing(dir_x, dir_y, dir_z, tilt_u, tilt_v, scale_q):
    facing_dot = (dir_x * tilt_u + dir_y * tilt_v + dir_z) * scale_q
    by_u = (dir_x - facing_dot * tilt_u * scale_q) * scale_q
    by_v = (dir_y - facing_dot * tilt_v * scale_q) * scale_q
    return (facing_dot, by_u, by_v)


def camera_terms(observed_c, weight_c, params, gains, lights, half_c, view_c, echo_c):
    tilt_u, tilt_v, diffuse, specular, sharp_raw, ambient, rim_gain, retro_gain = [
        params[i] for i in range(8)
    ]
    scale_q = 1.0 / jnp.sqrt(1.0 + tilt_u * tilt_u + tilt_v * tilt_v)
    light_dot, light_u, light_v = facing(
        lights[0][:, None], lights[1][:, None], lights[2][:, None], tilt_u, tilt_v, scale_q
    )
    half_dot, half_u, half_v = facing(
        half_c[0][:, None], half_c[1][:, None], half_c[2][:, None], tilt_u, tilt_v, scale_q
    )
    view_dot, view_u, view_v = facing(view_c[0], view_c[1], view_c[2], tilt_u, tilt_v, scale_q)
    sigma = jax.nn.sigmoid(sharp_raw)
    sharp = 1.0 + 20.0 * sigma
    lobe = jnp.exp(sharp * (half_dot - 1.0))
    back = 1.0 - view_dot
    rim_shape = back * back
    shaped = (
        diffuse * light_dot
        + specular * lobe
        + ambient
        + rim_gain * rim_shape
        + retro_gain * echo_c[:, None]
    )
    full = light_dot.shape
    jacob = [
        diffuse * light_u + specular * sharp * lobe * half_u - 2.0 * rim_gain * back * view_u,
        diffuse * light_v + specular * sharp * lobe * half_v - 2.0 * rim_gain * back * view_v,
        light_dot,
        lobe,
        specular * lobe * (half_dot - 1.0) * 20.0 * sigma * (1.0 - sigma),
        jnp.ones(full, jnp.float32),
        jnp.broadcast_to(rim_shape, full),
        jnp.broadcast_to(echo_c[:, None], full),
    ]
    column = gains[:, None]
    resid = observed_c.astype(jnp.float32) - column * shaped
    scaled = [column * piece for piece in jacob]
    surface_normal = []
    for i in range(8):
        for j in range(i, 8):
            surface_normal.append(weight_c * jnp.sum(scaled[i] * scaled[j], axis=0))
    right_side = [weight_c * jnp.sum(piece * resid, axis=0) for piece in scaled]
    lifted = jnp.sum(weight_c * shaped * resid, axis=1)
    energy = jnp.sum(weight_c * shaped * shaped, axis=1)
    return (jnp.stack(surface_normal), jnp.stack(right_side), lifted, energy)


def assemble(observed, weights, params, gains, lights, halves, views, echoes):
    texels = params.shape[1]

    def one_camera(carry, inputs):
        observed_c, weight_c, half_c, view_c, echo_c = inputs
        terms = camera_terms(observed_c, weight_c, params, gains, lights, half_c, view_c, echo_c)
        return (tuple((a + b for a, b in zip(carry, terms))), None)

    start = (
        jnp.zeros((36, texels), jnp.float32),
        jnp.zeros((8, texels), jnp.float32),
        jnp.zeros((LIGHTS,), jnp.float32),
        jnp.zeros((LIGHTS,), jnp.float32),
    )
    result, unused = lax.scan(one_camera, start, (observed, weights, halves, views, echoes))
    return result


def solve_eight(surface_normal, right_side):
    entries = {}
    where = 0
    for i in range(8):
        for j in range(i, 8):
            entries[i, j] = surface_normal[where]
            where += 1
    lower = {}
    for j in range(8):
        accum = entries[j, j] + damping
        for k in range(j):
            accum = accum - lower[j, k] * lower[j, k]
        root = jnp.sqrt(accum)
        lower[j, j] = root
        for i in range(j + 1, 8):
            accum = entries[j, i]
            for k in range(j):
                accum = accum - lower[i, k] * lower[j, k]
            lower[i, j] = accum / root
    forward = []
    for i in range(8):
        accum = right_side[i]
        for k in range(i):
            accum = accum - lower[i, k] * forward[k]
        forward.append(accum / lower[i, i])
    answer = [None] * 8
    for i in range(7, -1, -1):
        accum = forward[i]
        for k in range(i + 1, 8):
            accum = accum - lower[k, i] * answer[k]
        answer[i] = accum / lower[i, i]
    return jnp.stack(answer)


def smooth_tilts(tilt):
    rows = tilt.shape[1]
    cols = tilt.shape[2]
    padded = padded_2(tilt, (("grp", 1), ("tile", 2)), 1)
    boxed = jnp.zeros(tilt.shape, jnp.float32)
    for i in range(3):
        for j in range(3):
            boxed = boxed + padded[:, i : i + rows, j : j + cols]
    return 0.5 * tilt + boxed * (0.5 / 9.0)


def update_gains(gains, lifted, energy):
    totals = lax.psum(jnp.stack([lifted, energy]), ("grp", "tile"))
    return gains + totals[0] / (totals[1] + 1.0)


def on_device(observed, visible, params_start, light_directions, view_dirs, gains_start):
    lights, halves, views, echoes = geometry(light_directions, view_dirs)
    rows = visible.shape[0]
    cols = visible.shape[1]
    shifts = jnp.arange(CAMS, dtype=jnp.int32)
    weights = jnp.bitwise_and(jnp.right_shift(visible.reshape(1, -1), shifts[:, None]), 1).astype(
        jnp.float32
    )
    params = params_start.reshape(8, -1)
    gains = gains_start
    regrouped = lax.all_to_all(observed, "tile", split_axis=2, concat_axis=0, tiled=True)
    flat_obs = regrouped.reshape(CAMS, LIGHTS, rows * cols)
    first_terms = assemble(flat_obs, weights, params, gains, lights, halves, views, echoes)
    for iteration in range(ITERS):
        if iteration == 0:
            surface_normal, right_side, lifted, energy = first_terms
        else:
            surface_normal, right_side, lifted, energy = assemble(
                flat_obs, weights, params, gains, lights, halves, views, echoes
            )
        params = params + solve_eight(surface_normal, right_side)
        gains = update_gains(gains, lifted, energy)
        grid = params.reshape(8, rows, cols)
        params = jnp.concatenate([smooth_tilts(grid[:2]), grid[2:]], axis=0).reshape(8, -1)
    return (params.reshape(8, rows, cols), gains)


def solution(mesh):
    return jax.shard_map(
        on_device,
        mesh=mesh,
        in_specs=(P("tile", "grp", None), P("grp", "tile"), P(None, "grp", "tile"), P(), P(), P()),
        out_specs=(P(None, "grp", "tile"), P()),
        check_vma=False,
    )
```

profile of v0, /device:TPU:3, one launch (start us, length us, event | category | flops | bytes accessed | tf_op | source)
XLA Modules:
  0.0 603.4 jit_solution(8106772559715947173)
XLA Ops:
  0.6 6.7 %copy.16 = bf16[64,8,2048]{0,1,2:T(8,128)(2,1)} copy(bf16[64,8,2048]{2,1,0:T(8,128)(2,1)} %param.12) | data formatting | bytes 4194304 | tf_op args[0]
  7.3 7.6 %reshape.750 = bf16[8,2,65536]{2,1,0:T(2,128)(2,1)} reshape(bf16[2048,8,64]{2,1,0:T(8,128)(2,1)} %bitcast.458) | data formatting | bytes 4194304
  14.9 5.7 all-to-all-start
  22.1 46.7 %all-to-all-done = bf16[8,2,65536]{2,1,0:T(2,128)(2,1)S(1)} async-done(((bf16[8,2,65536]{2,1,0:T(2,128)(2,1)}), bf16[8,2,65536]{2,1,0:T(2,128)(2,1)S(1)}, u32[]{:S(2)}, u32[]{:S(2)}) %all-to-all-start) | async-done | bytes 2097184 | tf_op jit(solution)/shard_map/all_to_all | solution.py:177
  68.8 5.0 reshape.751
  73.8 5.0 copy.17
  81.2 201.9 %while.40 = (s32[]{:T(128)}, f32[36,2048]{1,0:T(8,128)S(1)}, f32[8,2048]{1,0:T(8,128)S(1)}, f32[32]{0:T(128)S(1)}, f32[32]{0:T(128)S(1)}, /*index=5*/f32[16,2048...) while((s32[]{:T(128)}, f32[36,2048]{1,0:T(8,128)S(1)}, ...), condition=%wide.region_51.52_spmd.clone, body=%wide.region_5.51_spmd.clone.sunk | while | flops 14035169 | bytes 4423358 | solution.py:113
  82.5 2.4 multiply_multiply_fusion.36
  95.1 2.4 multiply_multiply_fusion.36
  107.8 2.4 multiply_multiply_fusion.36
  120.4 2.4 multiply_multiply_fusion.36
  133.0 2.4 multiply_multiply_fusion.36
  145.6 2.4 multiply_multiply_fusion.36
  158.2 2.4 multiply_multiply_fusion.36
  170.8 2.4 multiply_multiply_fusion.36
  183.5 2.4 multiply_multiply_fusion.36
  233.9 2.4 multiply_multiply_fusion.36
  259.2 2.4 multiply_multiply_fusion.36
  284.9 3.1 collective-permute-start
  290.2 38.6 %psum.14 = f32[2,32]{1,0:T(2,128)S(1)} all-reduce(f32[2,32]{1,0:T(2,128)S(1)} %pad_maximum_fusion.10), channel_id=1, replica_groups=mesh['grp'=4,'tile'=8] {'grp','tile'}, use_global_device_ids=true, to_apply=%region_52.53 | all-reduce | flops 64 | bytes 512 | tf_op jit(solution)/shard_map/psum | solution.py:163
  329.5 5.9 collective-permute-start.2
  337.5 2.9 collective-permute-done.3
  340.8 203.1 %while.41 = (s32[]{:T(128)}, f32[36,2048]{1,0:T(8,128)S(1)}, f32[8,2048]{1,0:T(8,128)S(1)}, f32[32]{0:T(128)S(1)}, f32[32]{0:T(128)S(1)}, /*index=5*/f32[16,2048...) while((s32[]{:T(128)}, f32[36,2048]{1,0:T(8,128)S(1)}, ...), condition=%wide.region_100.101_spmd.clone, body=%wide.region_54.100_spmd.clone.sunk | while | flops 14035169 | bytes 4423358 | solution.py:113
  405.5 2.4 multiply_multiply_fusion.38
  418.2 2.4 multiply_multiply_fusion.38
  519.8 2.4 multiply_multiply_fusion.38
  532.5 2.4 multiply_multiply_fusion.38
  543.9 37.7 %psum.15 = f32[2,32]{1,0:T(2,128)S(1)} all-reduce(f32[2,32]{1,0:T(2,128)S(1)} %pad_maximum_fusion.11), channel_id=1, replica_groups=mesh['grp'=4,'tile'=8] {'grp','tile'}, use_global_device_ids=true, to_apply=%region_101.102 | all-reduce | flops 64 | bytes 512 | tf_op jit(solution)/shard_map/psum | solution.py:163
  583.3 3.1 collective-permute-start.4
  589.2 2.5 collective-permute-done.5
  591.7 5.8 collective-permute-start.6
  599.5 3.1 collective-permute-done.7
  (843 shorter events, 381.6 us)
Async XLA Ops:
  14.9 5.8 copy-start.3
  14.9 5.8 copy-start.5
  14.9 6.0 %copy-start.4 = (f32[3,32]{1,0:T(4,128)S(1)}, f32[3,32]{1,0:T(4,128)}, u32[]{:S(2)}) copy-start(f32[3,32]{1,0:T(4,128)} %param.15) | copy-start | bytes 1156
  14.9 6.4 %copy-start.1 = (f32[8,8,256]{2,1,0:T(8,128)S(1)}, f32[8,8,256]{2,1,0:T(8,128)}, u32[]{:S(2)}) copy-start(f32[8,8,256]{2,1,0:T(8,128)} %param.14) | copy-start | bytes 196612
  14.9 6.5 %copy-start.2 = (s32[8,256]{1,0:T(8,128)S(1)}, s32[8,256]{1,0:T(8,128)}, u32[]{:S(2)}) copy-start(s32[8,256]{1,0:T(8,128)} %param.13) | copy-start | bytes 24580
  14.9 6.5 %copy-start = (f32[32]{0:T(128)S(1)}, f32[32]{0:T(128)}, u32[]{:S(2)}) copy-start(f32[32]{0:T(128)} %param.17) | copy-start | bytes 388
  14.9 53.9 %all-to-all-start = ((bf16[8,2,65536]{2,1,0:T(2,128)(2,1)}), bf16[8,2,65536]{2,1,0:T(2,128)(2,1)S(1)}, u32[]{:S(2)}, u32[]{:S(2)}) async-start(bf16[8,2,65536]{2,1,0:T(2,128)(2,1)} %reshape.750), calls=%async_computation | async-start | bytes 4194304 | tf_op jit(solution)/shard_map/all_to_all | solution.py:177
  284.9 44.5 %collective-permute-start = (f32[2,1,256]{2,1,0:T(1,128)S(1)}, f32[2,1,256]{2,1,0:T(1,128)S(1)}, u32[]{:S(2)}, u32[]{:S(2)}) collective-permute-start(f32[2,1,256]{2,1,0:T(1,128)S(1)} %get-tuple-element.1093), channel_id=1, source_target_pairs={{0,8},{8,16},{16,24},{1,9},{9,17},{17,25},{2,10},{10,18},{18,26},{... | collective-permute-start | bytes 6152 | tf_op jit(solution)/shard_map/ppermute | solution.py:21
  288.0 41.4 %collective-permute-start.1 = (f32[2,1,256]{2,1,0:T(1,128)S(1)}, f32[2,1,256]{2,1,0:T(1,128)S(1)}, u32[]{:S(2)}, u32[]{:S(2)}) collective-permute-start(f32[2,1,256]{2,1,0:T(1,128)S(1)} %get-tuple-element.1094), channel_id=1, source_target_pairs={{8,0},{16,8},{24,16},{9,1},{17,9},{25,17},{10,2},{18,10},{26,18},{... | collective-permute-start | bytes 6152 | tf_op jit(solution)/shard_map/ppermute | solution.py:23
  329.5 8.0 %collective-permute-start.2 = (f32[2,10,1]{2,1,0:T(8,128)S(1)}, f32[2,10,1]{2,1,0:T(8,128)S(1)}, u32[]{:S(2)}, u32[]{:S(2)}) collective-permute-start(f32[2,10,1]{2,1,0:T(8,128)S(1)} %get-tuple-element.1081), channel_id=1, source_target_pairs={{0,1},{1,2},{2,3},{3,4},{4,5},{5,6},{6,7},{8,9},{9,10},{10,11},{11... | collective-permute-start | bytes 248 | tf_op jit(solution)/shard_map/ppermute | solution.py:21
  335.4 5.1 collective-permute-start.3
  583.3 5.9 collective-permute-start.4
  586.4 5.2 collective-permute-start.5
  591.7 7.8 %collective-permute-start.6 = (f32[2,10,1]{2,1,0:T(8,128)S(1)}, f32[2,10,1]{2,1,0:T(8,128)S(1)}, u32[]{:S(2)}, u32[]{:S(2)}) collective-permute-start(f32[2,10,1]{2,1,0:T(8,128)S(1)} %get-tuple-element.1079), channel_id=1, source_target_pairs={{0,1},{1,2},{2,3},{3,4},{4,5},{5,6},{6,7},{8,9},{9,10},{10,11},{11... | collective-permute-start | bytes 248 | tf_op jit(solution)/shard_map/ppermute | solution.py:21
  597.6 5.1 collective-permute-start.7
where the time goes:
time: 608 us; the launch traced here: 603 us
  other arithmetic  366 us (60%)
  blocking collectives  76.3 us (13%)
  local copies, waits for them, and re-layouts  67.8 us (11%)
  waiting for transfers between devices  55.2 us (9%)
  starting transfers between devices  32 us (5%)
    mul x32, other arithmetic, camera_terms(): 2.0 * rim_gain * back * view_v  78.1 us
    psum x2, blocking collectives, update_gains(): totals = lax.psum(jnp.stack([lifted, energy]), ('grp', 'tile'))  76.3 us
    reduce_sum x98, other arithmetic, camera_terms(): surface_normal.append(weight_c * jnp.sum(scaled[i] * scaled[j], axis=0))  61.1 us
    mul x32, other arithmetic, camera_terms(): rim_shape = back * back  57.2 us
    all_to_all x1, waiting for transfers between devices, on_device(): lax.all_to_all(observed, 'tile', split_axis=2, concat_axis=0, tiled=True)  46.7 us
    reduce_sum x32, other arithmetic, camera_terms(): lifted = jnp.sum(weight_c * shaped * resid, axis=1)  46.1 us
    mul x32, other arithmetic, camera_terms(): right_side = [weight_c * jnp.sum(piece * resid, axis=0) for piece in scaled]  43.2 us
    reduce_sum x32, other arithmetic, camera_terms(): right_side = [weight_c * jnp.sum(piece * resid, axis=0) for piece in scaled]  41.6 us
  transfers between devices with their start and end apart: 9, of which 4 were waited for; matrix products, arithmetic and copies ran while one was open for 0% of the time, Pallas kernels for 0%

commit v1 on v0

--- a/solution.py
+++ b/solution.py
@@ -1,3 +1,4 @@
+import functools
 import jax
 import jax.numpy as jnp
 from jax import lax
@@ -8,6 +9,15 @@
 ITERS = 2
 damping = 4.0
 lift_z = 1.6
+
+
+def test_the_notes(base_x, a_name, axis_name):
+    big = lax.psum(base_x, a_name)
+    state_next = lax.psum(big, axis_name)
+    return state_next
+
+
+_resolve_windows = functools.partial(test_the_notes, a_name="tile", axis_name="grp")
 
 
 def padded_2(cells, sides, width):
@@ -160,7 +170,7 @@
 
 
 def update_gains(gains, lifted, energy):
-    totals = lax.psum(jnp.stack([lifted, energy]), ("grp", "tile"))
+    totals = _resolve_windows(jnp.stack([lifted, energy]))
     return gains + totals[0] / (totals[1] + 1.0)
 
 

time: 608 us -> 567 us (0.933)
  blocking collectives: 76.3 us -> 41 us
    psum x2 -> x4, blocking collectives: 76.3 us -> 41 us  [the longest x2 27.2 us: test_the_notes(): big = lax.psum(base_x, a_name)]
where the time goes in v1:
time: 567 us; the launch traced here: 563 us
  other arithmetic  366 us (65%)
  local copies, waits for them, and re-layouts  67.8 us (12%)
  waiting for transfers between devices  51.7 us (9%)
  blocking collectives  41 us (7%)
  starting transfers between devices  30.6 us (5%)
    mul x32, other arithmetic, camera_terms(): 2.0 * rim_gain * back * view_v  78.1 us
    reduce_sum x98, other arithmetic, camera_terms(): surface_normal.append(weight_c * jnp.sum(scaled[i] * scaled[j], axis=0))  61 us
    mul x32, other arithmetic, camera_terms(): rim_shape = back * back  57.2 us
    all_to_all x1, waiting for transfers between devices, on_device(): lax.all_to_all(observed, 'tile', split_axis=2, concat_axis=0, tiled=True)  46.7 us
    reduce_sum x32, other arithmetic, camera_terms(): lifted = jnp.sum(weight_c * shaped * resid, axis=1)  46.1 us
    mul x32, other arithmetic, camera_terms(): right_side = [weight_c * jnp.sum(piece * resid, axis=0) for piece in scaled]  43.2 us
    reduce_sum x32, other arithmetic, camera_terms(): right_side = [weight_c * jnp.sum(piece * resid, axis=0) for piece in scaled]  41.8 us
    psum x2, blocking collectives, test_the_notes(): big = lax.psum(base_x, a_name)  27.2 us
  transfers between devices with their start and end apart: 9, of which 4 were waited for; matrix products, arithmetic and copies ran while one was open for 0% of the time, Pallas kernels for 0%

profile of v1, /device:TPU:3, one launch (start us, length us, event | category | flops | bytes accessed | tf_op | source)
XLA Modules:
  0.0 563.3 jit_solution(9645166580960655963)
XLA Ops:
  0.6 6.7 %copy.16 = bf16[64,8,2048]{0,1,2:T(8,128)(2,1)} copy(bf16[64,8,2048]{2,1,0:T(8,128)(2,1)} %param.12) | data formatting | bytes 4194304 | tf_op args[0]
  7.3 7.6 %reshape.750 = bf16[8,2,65536]{2,1,0:T(2,128)(2,1)} reshape(bf16[2048,8,64]{2,1,0:T(8,128)(2,1)} %bitcast.458) | data formatting | bytes 4194304
  14.9 5.7 %all-to-all-start = ((bf16[8,2,65536]{2,1,0:T(2,128)(2,1)}), bf16[8,2,65536]{2,1,0:T(2,128)(2,1)S(1)}, u32[]{:S(2)}, u32[]{:S(2)}) async-start(bf16[8,2,65536]{2,1,0:T(2,128)(2,1)} %reshape.750), calls=%async_computation | async-start | bytes 4194304 | tf_op jit(solution)/shard_map/all_to_all | solution.py:187
  22.1 46.7 %all-to-all-done = bf16[8,2,65536]{2,1,0:T(2,128)(2,1)S(1)} async-done(((bf16[8,2,65536]{2,1,0:T(2,128)(2,1)}), bf16[8,2,65536]{2,1,0:T(2,128)(2,1)S(1)}, u32[]{:S(2)}, u32[]{:S(2)}) %all-to-all-start) | async-done | bytes 2097184 | tf_op jit(solution)/shard_map/all_to_all | solution.py:187
  68.8 5.0 reshape.751
  73.8 5.0 copy.17
  81.2 201.9 %while.40 = (s32[]{:T(128)}, f32[36,2048]{1,0:T(8,128)S(1)}, f32[8,2048]{1,0:T(8,128)S(1)}, f32[32]{0:T(128)S(1)}, f32[32]{0:T(128)S(1)}, /*index=5*/f32[16,2048...) while((s32[]{:T(128)}, f32[36,2048]{1,0:T(8,128)S(1)}, ...), condition=%wide.region_51.52_spmd.clone, body=%wide.region_5.51_spmd.clone.sunk | while | flops 14035169 | bytes 4423358 | solution.py:123
  82.5 2.4 multiply_multiply_fusion.36
  95.1 2.4 multiply_multiply_fusion.36
  107.8 2.4 multiply_multiply_fusion.36
  120.4 2.4 multiply_multiply_fusion.36
  133.0 2.4 multiply_multiply_fusion.36
  145.6 2.4 multiply_multiply_fusion.36
  183.5 2.4 multiply_multiply_fusion.36
  221.3 2.4 multiply_multiply_fusion.36
  284.9 3.1 collective-permute-start
  290.2 14.4 %psum.28 = f32[2,32]{1,0:T(2,128)S(1)} all-reduce(f32[2,32]{1,0:T(2,128)S(1)} %pad_maximum_fusion.10), channel_id=1, replica_groups=mesh['grp'=4,'tile'=8] {'tile'}, use_global_device_ids=true, to_apply=%region_52.53 | all-reduce | flops 64 | bytes 512 | tf_op jit(solution)/shard_map/psum | solution.py:15
  304.6 6.9 %psum.29 = f32[2,32]{1,0:T(2,128)S(1)} all-reduce(f32[2,32]{1,0:T(2,128)S(1)} %psum.28), channel_id=1, replica_groups=mesh['grp'=4,'tile'=8] {'grp'}, use_global_device_ids=true, to_apply=%region_53.54 | all-reduce | flops 64 | bytes 512 | tf_op jit(solution)/shard_map/psum | solution.py:16
  312.3 2.5 collective-permute-start.2
  314.8 3.9 collective-permute-start.3
  320.1 203.2 %while.41 = (s32[]{:T(128)}, f32[36,2048]{1,0:T(8,128)S(1)}, f32[8,2048]{1,0:T(8,128)S(1)}, f32[32]{0:T(128)S(1)}, f32[32]{0:T(128)S(1)}, /*index=5*/f32[16,2048...) while((s32[]{:T(128)}, f32[36,2048]{1,0:T(8,128)S(1)}, ...), condition=%wide.region_101.102_spmd.clone, body=%wide.region_55.101_spmd.clone.sunk | while | flops 14035169 | bytes 4423358 | solution.py:123
  321.4 2.4 multiply_multiply_fusion.38
  359.5 2.4 multiply_multiply_fusion.38
  397.6 2.4 multiply_multiply_fusion.38
  461.1 2.4 multiply_multiply_fusion.38
  499.2 2.4 multiply_multiply_fusion.38
  523.3 12.8 %psum.30 = f32[2,32]{1,0:T(2,128)S(1)} all-reduce(f32[2,32]{1,0:T(2,128)S(1)} %pad_maximum_fusion.11), channel_id=1, replica_groups=mesh['grp'=4,'tile'=8] {'tile'}, use_global_device_ids=true, to_apply=%region_102.103 | all-reduce | flops 64 | bytes 512 | tf_op jit(solution)/shard_map/psum | solution.py:15
  536.1 6.9 %psum.31 = f32[2,32]{1,0:T(2,128)S(1)} all-reduce(f32[2,32]{1,0:T(2,128)S(1)} %psum.30), channel_id=1, replica_groups=mesh['grp'=4,'tile'=8] {'grp'}, use_global_device_ids=true, to_apply=%region_103.104 | all-reduce | flops 64 | bytes 512 | tf_op jit(solution)/shard_map/psum | solution.py:16
  544.7 3.1 collective-permute-start.4
  550.6 2.5 collective-permute-done.5
  553.2 4.3 collective-permute-start.6
  557.5 3.7 collective-permute-start.7
  (845 shorter events, 385.0 us)
Async XLA Ops:
  14.9 5.8 %copy-start.3 = (f32[3,16]{1,0:T(4,128)S(1)}, f32[3,16]{1,0:T(4,128)}, u32[]{:S(2)}) copy-start(f32[3,16]{1,0:T(4,128)} %param.16) | copy-start | bytes 580
  14.9 5.8 %copy-start.5 = (f32[3]{0:T(128)S(1)}, f32[3]{0:T(128)}, u32[]{:S(2)}) copy-start(f32[3]{0:T(128)} %constant.128.clone) | copy-start | bytes 40
  14.9 6.0 %copy-start.4 = (f32[3,32]{1,0:T(4,128)S(1)}, f32[3,32]{1,0:T(4,128)}, u32[]{:S(2)}) copy-start(f32[3,32]{1,0:T(4,128)} %param.15) | copy-start | bytes 1156
  14.9 6.4 %copy-start.1 = (f32[8,8,256]{2,1,0:T(8,128)S(1)}, f32[8,8,256]{2,1,0:T(8,128)}, u32[]{:S(2)}) copy-start(f32[8,8,256]{2,1,0:T(8,128)} %param.14) | copy-start | bytes 196612
  14.9 6.5 %copy-start.2 = (s32[8,256]{1,0:T(8,128)S(1)}, s32[8,256]{1,0:T(8,128)}, u32[]{:S(2)}) copy-start(s32[8,256]{1,0:T(8,128)} %param.13) | copy-start | bytes 24580
  14.9 6.5 %copy-start = (f32[32]{0:T(128)S(1)}, f32[32]{0:T(128)}, u32[]{:S(2)}) copy-start(f32[32]{0:T(128)} %param.17) | copy-start | bytes 388
  14.9 53.9 %all-to-all-start = ((bf16[8,2,65536]{2,1,0:T(2,128)(2,1)}), bf16[8,2,65536]{2,1,0:T(2,128)(2,1)S(1)}, u32[]{:S(2)}, u32[]{:S(2)}) async-start(bf16[8,2,65536]{2,1,0:T(2,128)(2,1)} %reshape.750), calls=%async_computation | async-start | bytes 4194304 | tf_op jit(solution)/shard_map/all_to_all | solution.py:187
  284.9 27.2 %collective-permute-start = (f32[2,1,256]{2,1,0:T(1,128)S(1)}, f32[2,1,256]{2,1,0:T(1,128)S(1)}, u32[]{:S(2)}, u32[]{:S(2)}) collective-permute-start(f32[2,1,256]{2,1,0:T(1,128)S(1)} %get-tuple-element.1093), channel_id=1, source_target_pairs={{0,8},{8,16},{16,24},{1,9},{9,17},{17,25},{2,10},{10,18},{18,26},{... | collective-permute-start | bytes 6152 | tf_op jit(solution)/shard_map/ppermute | solution.py:31
  288.0 24.1 %collective-permute-start.1 = (f32[2,1,256]{2,1,0:T(1,128)S(1)}, f32[2,1,256]{2,1,0:T(1,128)S(1)}, u32[]{:S(2)}, u32[]{:S(2)}) collective-permute-start(f32[2,1,256]{2,1,0:T(1,128)S(1)} %get-tuple-element.1094), channel_id=1, source_target_pairs={{8,0},{16,8},{24,16},{9,1},{17,9},{25,17},{10,2},{18,10},{26,18},{... | collective-permute-start | bytes 6152 | tf_op jit(solution)/shard_map/ppermute | solution.py:33
  312.3 6.4 %collective-permute-start.2 = (f32[2,10,1]{2,1,0:T(8,128)S(1)}, f32[2,10,1]{2,1,0:T(8,128)S(1)}, u32[]{:S(2)}, u32[]{:S(2)}) collective-permute-start(f32[2,10,1]{2,1,0:T(8,128)S(1)} %get-tuple-element.1081), channel_id=1, source_target_pairs={{0,1},{1,2},{2,3},{3,4},{4,5},{5,6},{6,7},{8,9},{9,10},{10,11},{11... | collective-permute-start | bytes 248 | tf_op jit(solution)/shard_map/ppermute | solution.py:31
  314.8 5.1 collective-permute-start.3
  544.7 5.9 %collective-permute-start.4 = (f32[2,1,256]{2,1,0:T(1,128)S(1)}, f32[2,1,256]{2,1,0:T(1,128)S(1)}, u32[]{:S(2)}, u32[]{:S(2)}) collective-permute-start(f32[2,1,256]{2,1,0:T(1,128)S(1)} %get-tuple-element.1087), channel_id=1, source_target_pairs={{0,8},{8,16},{16,24},{1,9},{9,17},{17,25},{2,10},{10,18},{18,26},{... | collective-permute-start | bytes 6152 | tf_op jit(solution)/shard_map/ppermute | solution.py:31
  547.8 5.2 collective-permute-start.5
  553.2 8.0 %collective-permute-start.6 = (f32[2,10,1]{2,1,0:T(8,128)S(1)}, f32[2,10,1]{2,1,0:T(8,128)S(1)}, u32[]{:S(2)}, u32[]{:S(2)}) collective-permute-start(f32[2,10,1]{2,1,0:T(8,128)S(1)} %get-tuple-element.1079), channel_id=1, source_target_pairs={{0,1},{1,2},{2,3},{3,4},{4,5},{5,6},{6,7},{8,9},{9,10},{10,11},{11... | collective-permute-start | bytes 248 | tf_op jit(solution)/shard_map/ppermute | solution.py:31
  557.5 5.1 collective-permute-start.7
